TPU v7x, 768 devices: a whole 4x8x12 slice. The times are simulated.
768 devices in a mesh: rows: 96 (over z, y), heads: 8 (over x, core).
Axes of the slice: x: 4, y: 8, z: 12, core: 2. Of those that a mesh axis runs over, the one named last changes fastest.
Arguments:
- queries: bfloat16 [49152, 1024], P('rows', 'heads'), may hold values from -6 to 6
- key_vectors: bfloat16 [49152, 1024], P('rows', 'heads'), may hold values from -6 to 6
- value_vectors: bfloat16 [49152, 1024], P('rows', 'heads'), may hold values from -120 to 120
- gating: bfloat16 [49152, 1024], P('rows', 'heads'), may hold values from -6 to 6
- bounds: int32 [2, 49152], P(None, 'rows'), may hold values from 0 to 49151, as said below
- cotangent: bfloat16 [49152, 1024], P('rows', 'heads'), may hold values from -6 to 6
Outputs:
- layer_out: bfloat16 [49152, 1024], P('rows', 'heads')
- grad_queries: bfloat16 [49152, 1024], P('rows', 'heads')
- grad_keys: bfloat16 [49152, 1024], P('rows', 'heads')
- grad_values: bfloat16 [49152, 1024], P('rows', 'heads')
- grad_gating: bfloat16 [49152, 1024], P('rows', 'heads')
Inputs may be any that keep to these rules, and one draw needn't show every extreme that they name: bounds[0, r] and bounds[1, r] are the first and the last row of the history that holds row r; histories are runs of consecutive rows that cover all 49152 rows, each at most 1024 rows long, and one of them exactly that long.
All inputs are finite; a program needn't handle non-finite values.
Results may differ from a plain program's by a relative error of at most 0.006.
Values may be sent and summed in bfloat16 or wider, within the bound.
A program may use at most 32 MiB of HBM per device.

v0:
```python
import jax
import jax.numpy as jnp
from jax import lax
from jax.sharding import PartitionSpec as P

DH = 128
REACH = 2


EPSILON = 1e-05


def from_behind(value, axis, steps):
    count = lax.axis_size(axis)
    initial, last = (max(0, -steps), min(count, count - steps))
    return lax.ppermute(value, axis, [(source, source + steps) for source in range(initial, last)])


def silu_parts(query_tile, key_tile, allowed, factor):
    scores = (
        jnp.einsum("qhd,khd->hqk", query_tile, key_tile, preferred_element_type=jnp.float32)
        * factor
    )
    sigmoid = jax.nn.sigmoid(scores)
    weights = jnp.where(allowed[None], scores * sigmoid, 0.0).astype(jnp.bfloat16)
    return (scores, sigmoid, weights)


def tile_backward(query_part, key_part, value_part, delta_part, allowed, factor):
    scores, sigmoid, weights = silu_parts(query_part, key_part, allowed, factor)
    pulled = jnp.einsum("qhd,khd->hqk", delta_part, value_part, preferred_element_type=jnp.float32)
    score_grad = jnp.where(
        allowed[None], pulled * sigmoid * (1.0 + scores * (1.0 - sigmoid)), 0.0
    ).astype(jnp.bfloat16)
    query_add = jnp.einsum("hqk,khd->qhd", score_grad, key_part, preferred_element_type=jnp.float32)
    key_add = (
        jnp.einsum("hqk,qhd->khd", score_grad, query_part, preferred_element_type=jnp.float32)
        * factor
    )
    value_add = jnp.einsum("hqk,qhd->khd", weights, delta_part, preferred_element_type=jnp.float32)
    return (query_add, key_add, value_add)


def local(queries, key_vectors, value_vectors, gating, bounds, cotangent):
    rows_dev, feature_width = queries.shape
    heads_dev = feature_width // DH
    factor = DH ** (-0.5)
    features = feature_width * lax.axis_size("heads")
    position = lax.axis_index("rows")
    first_row = position * rows_dev
    local_rows = jnp.arange(rows_dev, dtype=jnp.int32)
    row_ids = first_row + local_rows
    starts = bounds[0]
    query_tile = queries.reshape(rows_dev, heads_dev, DH)
    key_tile = key_vectors.reshape(rows_dev, heads_dev, DH)
    value_tile = value_vectors.reshape(rows_dev, heads_dev, DH)
    empty_tile = jnp.zeros((rows_dev, heads_dev, DH), jnp.float32)
    neighbours = [(key_tile, value_tile)]
    for offset in range(1, REACH + 1):
        neighbours.append(from_behind((key_tile, value_tile), "rows", offset))

    def owner_mask(offset):
        key_ids = first_row - offset * rows_dev + local_rows
        return (key_ids[None, :] >= starts[:, None]) & (key_ids[None, :] <= row_ids[:, None])

    attended = empty_tile
    for offset in range(REACH + 1):
        key_part, value_part = neighbours[offset]
        allowed = owner_mask(offset)
        weights = silu_parts(query_tile, key_part, allowed, factor)[2]
        attended = attended + jnp.einsum(
            "hqk,khd->qhd", weights, value_part, preferred_element_type=jnp.float32
        )
    attended = attended.reshape(rows_dev, feature_width)
    total_sum, square_sum = lax.psum(
        (jnp.sum(attended, axis=1), jnp.sum(attended * attended, axis=1)), "heads"
    )
    average = total_sum[:, None] / features
    variance = square_sum[:, None] / features - average * average
    inverse = lax.rsqrt(variance + EPSILON)
    normed = (attended - average) * inverse
    gate_float = gating.astype(jnp.float32)
    layer_out = (normed * gate_float).astype(jnp.bfloat16)
    upstream = cotangent.astype(jnp.float32)
    grad_gating = (upstream * normed).astype(jnp.bfloat16)
    scaled = upstream * gate_float
    grad_sum, cross_sum = lax.psum(
        (jnp.sum(scaled, axis=1), jnp.sum(scaled * normed, axis=1)), "heads"
    )
    delta_rows = (
        inverse * (scaled - grad_sum[:, None] / features - normed * (cross_sum[:, None] / features))
    ).astype(jnp.bfloat16)
    delta_tile = delta_rows.reshape(rows_dev, heads_dev, DH)
    grad_query = empty_tile
    grad_key = empty_tile
    grad_value = empty_tile
    for offset in range(REACH + 1):
        key_part, value_part = neighbours[offset]
        allowed = owner_mask(offset)
        query_add, key_add, value_add = tile_backward(
            query_tile, key_part, value_part, delta_tile, allowed, factor
        )
        grad_query = grad_query + query_add
        if offset == 0:
            grad_key = key_add
            grad_value = value_add
        else:
            key_back, value_back = from_behind((key_add, value_add), "rows", -offset)
            grad_key = grad_key + key_back
            grad_value = grad_value + value_back
    grad_queries = (grad_query * factor).reshape(rows_dev, feature_width).astype(jnp.bfloat16)
    grad_keys = grad_key.reshape(rows_dev, feature_width).astype(jnp.bfloat16)
    grad_values = grad_value.reshape(rows_dev, feature_width).astype(jnp.bfloat16)
    return (layer_out, grad_queries, grad_keys, grad_values, grad_gating)


def solution(mesh):
    return jax.shard_map(
        local,
        mesh=mesh,
        in_specs=(
            P("rows", "heads"),
            P("rows", "heads"),
            P("rows", "heads"),
            P("rows", "heads"),
            P(None, "rows"),
            P("rows", "heads"),
        ),
        out_specs=(
            P("rows", "heads"),
            P("rows", "heads"),
            P("rows", "heads"),
            P("rows", "heads"),
            P("rows", "heads"),
        ),
        check_vma=False,
    )
```

profile of v0, /device:TPU:248, one launch (start us, length us, event | category | flops | bytes accessed | tf_op | source)
XLA Modules:
  0.0 100.5 jit_solution(16771270104015530621)
XLA Ops:
  0.6 4.8 %collective-permute-start = (bf16[512,1,128]{2,0,1:T(8,128)(2,1)}, bf16[512,1,128]{2,0,1:T(8,128)(2,1)S(1)}, u32[]{:S(2)}, u32[]{:S(2)}) collective-permute-start(bf16[512,1,128]{2,0,1:T(8,128)(2,1)} %bitcast.105), channel_id=1, source_target_pairs={{0,8},{8,16},{16,24},{24,32},{32,40},{40,48},{48,56},{56,64},{64,7... | collective-permute-start | bytes 393224 | tf_op jit(solution)/shard_map/ppermute | solution.py:16
  5.5 4.5 %collective-permute-start.2 = (bf16[512,1,128]{2,0,1:T(8,128)(2,1)}, bf16[512,1,128]{2,0,1:T(8,128)(2,1)S(1)}, u32[]{:S(2)}, u32[]{:S(2)}) collective-permute-start(bf16[512,1,128]{2,0,1:T(8,128)(2,1)} %bitcast.106), channel_id=1, source_target_pairs={{0,16},{8,24},{16,32},{24,40},{32,48},{40,56},{48,64},{56,72},{64,... | collective-permute-start | bytes 393224 | tf_op jit(solution)/shard_map/ppermute | solution.py:16
  10.0 3.5 %collective-permute-start.1 = (bf16[512,1,128]{2,0,1:T(8,128)(2,1)}, bf16[512,1,128]{2,0,1:T(8,128)(2,1)}, u32[]{:S(2)}, u32[]{:S(2)}) collective-permute-start(bf16[512,1,128]{2,0,1:T(8,128)(2,1)} %bitcast.107), channel_id=1, source_target_pairs={{0,8},{8,16},{16,24},{24,32},{32,40},{40,48},{48,56},{56,64},{64,7... | collective-permute-start | bytes 393224 | tf_op jit(solution)/shard_map/ppermute | solution.py:16
  13.5 4.8 %collective-permute-start.3 = (bf16[512,1,128]{2,0,1:T(8,128)(2,1)}, bf16[512,1,128]{2,0,1:T(8,128)(2,1)}, u32[]{:S(2)}, u32[]{:S(2)}) collective-permute-start(bf16[512,1,128]{2,0,1:T(8,128)(2,1)} %bitcast.108), channel_id=1, source_target_pairs={{0,16},{8,24},{16,32},{24,40},{32,48},{40,56},{48,64},{56,72},{64,... | collective-permute-start | bytes 393224 | tf_op jit(solution)/shard_map/ppermute | solution.py:16
  18.3 2.2 %convolution_multiply_fusion.5 = f32[512,512]{1,0:T(8,128)} fusion(bf16[512,128]{1,0:T(8,128)(2,1)S(1)} %copy-done, bf16[512,128]{1,0:T(8,128)(2,1)} %param.7), kind=kOutput, calls=%fused_computation.5 | convolution fusion | flops 67371008 | bytes 1310720 | tf_op jit(solution)/shard_map/qhd,khd->hqk/dot_general | solution.py:21
  20.6 0.7 copy-done.16
  21.4 0.8 copy-done.9
  22.9 0.6 copy-done.1
  23.5 2.2 %select_convert_fusion = (bf16[512,512]{1,0:T(8,128)(2,1)S(1)}, bf16[512,512]{1,0:T(8,128)(2,1)S(1)}, bf16[512,512]{1,0:T(8,128)(2,1)S(1)}, f32[512,512]{1,0:T(8,128)}) fusion(s32[512]{0:T(512)S(1)} %get-tuple-element.28, s32[512]{0:T(512)S(1)} %get-tuple-element.29, s32[512]{0:T(512)S(1)} %bitcast.109, f32[512,512]{1,0:T(8,128)S(1)} %convolution_multiply_fusion.4, ...), kind=kOutput, calls=%fused_computation.38 | convolution fusion | flops 74448896 | bytes 4988928 | tf_op jit(solution)/shard_map/qhd,khd->hqk/dot_general | solution.py:21
  26.0 1.2 %convolution_add_fusion.3 = f32[512,128]{0,1:T(8,128)S(1)} fusion(f32[512,128]{0,1:T(8,128)S(1)} %fusion.34, bf16[512,512]{1,0:T(8,128)(2,1)S(1)} %get-tuple-element.22, bf16[512,1,128]{2,0,1:T(8,128)(2,1)} %collective-permute-done.1), kind=kOutput, calls=%fused_computation.27 | convolution fusion | flops 67174400 | bytes 1179648 | tf_op jit(solution)/shard_map/hqk,khd->qhd/dot_general | solution.py:71
  27.2 1.2 %fusion.33 = (f32[512]{0:T(512)S(1)}, f32[512]{0:T(512)S(1)}, f32[512,128]{0,1:T(8,128)S(1)}) fusion(f32[512,128]{0,1:T(8,128)S(1)} %convolution_add_fusion.3, bf16[512,512]{1,0:T(8,128)(2,1)S(1)} %get-tuple-element.21, bf16[512,1,128]{2,0,1:T(8,128)(2,1)} %collective-permute-done.3), kind=kOutput, calls=%fused_computation.72 | convolution fusion | flops 67369984 | bytes 1183744 | tf_op jit(solution)/shard_map/hqk,khd->qhd/dot_general | solution.py:71
  28.5 13.5 %all-reduce.1 = (f32[512]{0:T(512)S(1)}, f32[512]{0:T(512)S(1)}) all-reduce(f32[512]{0:T(512)S(1)} %get-tuple-element.13, f32[512]{0:T(512)S(1)} %get-tuple-element.12), channel_id=1, replica_groups=mesh['rows'=96,'heads'=8] {'heads'}, use_global_device_ids=true, to_apply=%region_3.4 | all-reduce | flops 1024 | bytes 8192 | tf_op jit(solution)/shard_map/psum | solution.py:75
  42.1 12.4 %all-reduce = (f32[512]{0:T(512)S(1)}, f32[512]{0:T(512)S(1)}) all-reduce(f32[512]{0:T(512)S(1)} %get-tuple-element.11, f32[512]{0:T(512)S(1)} %get-tuple-element.10), channel_id=1, replica_groups=mesh['rows'=96,'heads'=8] {'heads'}, use_global_device_ids=true, to_apply=%region_7.8 | all-reduce | flops 1024 | bytes 8192 | tf_op jit(solution)/shard_map/psum | solution.py:87
  54.5 0.8 fusion.23
  55.3 0.9 convolution_bitcast_fusion.1
  57.3 0.6 fusion.8
  57.9 3.2 %collective-permute-start.6 = (f32[512,1,128]{0,2,1:T(8,128)}, f32[512,1,128]{0,2,1:T(8,128)S(1)}, u32[]{:S(2)}, u32[]{:S(2)}) collective-permute-start(f32[512,1,128]{0,2,1:T(8,128)} %convolution_bitcast_fusion.1), channel_id=1, source_target_pairs={{8,0},{16,8},{24,16},{32,24},{40,32},{48,40},{56,48},{64,56},{72,6... | collective-permute-start | bytes 786440 | tf_op jit(solution)/shard_map/ppermute | solution.py:16
  61.2 1.9 %collective-permute-start.7 = (f32[512,1,128]{0,2,1:T(8,128)S(1)}, f32[512,1,128]{0,2,1:T(8,128)}, u32[]{:S(2)}, u32[]{:S(2)}) collective-permute-start(f32[512,1,128]{0,2,1:T(8,128)S(1)} %convolution_bitcast_fusion), channel_id=1, source_target_pairs={{16,0},{24,8},{32,16},{40,24},{48,32},{56,40},{64,48},{72,56},{80,... | collective-permute-start | bytes 786440 | tf_op jit(solution)/shard_map/ppermute | solution.py:16
  63.1 1.5 %fusion.6 = bf16[512,512]{1,0:T(8,128)(2,1)S(1)} fusion(bf16[512,128]{0,1:T(8,128)(2,1)S(1)} %get-tuple-element.19, f32[512,512]{1,0:T(8,128)S(1)} %copy-done.17, s32[512]{0:T(512)S(1)} %copy-done.15, s32[512]{0:T(512)S(1)} %copy-done.13, s32[512]{0:T(512)S(1)} %bitcast.111, bf16[512,1,128]{2,0,1:T(8,128)(2,1)} %collective-permute-done.3), kind=kOutput, calls=%fused_computation.12 | convolution fusion | flops 70516736 | bytes 1841152 | tf_op jit(solution)/shard_map/qhd,khd->hqk/dot_general | solution.py:31
  64.7 1.0 %fusion.9 = f32[512,1,128]{2,0,1:T(8,128)} fusion(bf16[512,512]{1,0:T(8,128)(2,1)S(1)} %fusion.6, bf16[512,128]{1,0:T(8,128)(2,1)S(1)} %copy-done), kind=kOutput, calls=%fused_computation.19 | convolution fusion | flops 67174400 | bytes 917504 | tf_op jit(solution)/shard_map/hqk,qhd->khd/dot_general | solution.py:37
  65.7 2.6 %collective-permute-start.5 = (f32[512,1,128]{2,0,1:T(8,128)}, f32[512,1,128]{2,0,1:T(8,128)S(1)}, u32[]{:S(2)}, u32[]{:S(2)}) collective-permute-start(f32[512,1,128]{2,0,1:T(8,128)} %fusion.9), channel_id=1, source_target_pairs={{16,0},{24,8},{32,16},{40,24},{48,32},{56,40},{64,48},{72,56},{80,... | collective-permute-start | bytes 786440 | tf_op jit(solution)/shard_map/ppermute | solution.py:16
  68.3 1.5 %fusion.7 = bf16[512,512]{1,0:T(8,128)(2,1)S(1)} fusion(bf16[512,128]{0,1:T(8,128)(2,1)S(1)} %get-tuple-element.19, f32[512,512]{1,0:T(8,128)S(1)} %convolution_multiply_fusion.4, s32[512]{0:T(512)S(1)} %iota_add_fusion.1, s32[512]{0:T(512)S(1)} %copy-done.13, s32[512]{0:T(512)S(1)} %bitcast.112, bf16[512,1,128]{2,0,1:T(8,128)(2,1)} %collective-permute-done.1), kind=kOutput, calls=%fused_computation.13 | convolution fusion | flops 70516736 | bytes 1841152 | tf_op jit(solution)/shard_map/qhd,khd->hqk/dot_general | solution.py:31
  70.2 2.0 %collective-permute-start.4 = (f32[512,1,128]{2,0,1:T(8,128)S(1)}, f32[512,1,128]{2,0,1:T(8,128)S(1)}, u32[]{:S(2)}, u32[]{:S(2)}) collective-permute-start(f32[512,1,128]{2,0,1:T(8,128)S(1)} %fusion.10), channel_id=1, source_target_pairs={{8,0},{16,8},{24,16},{32,24},{40,32},{48,40},{56,48},{64,56},{72,6... | collective-permute-start | bytes 786440 | tf_op jit(solution)/shard_map/ppermute | solution.py:16
  73.4 1.0 fusion.18
  74.4 0.8 copy.13
  75.3 0.8 copy.15
  76.1 8.0 %collective-permute-done.7 = f32[512,1,128]{0,2,1:T(8,128)} collective-permute-done((f32[512,1,128]{0,2,1:T(8,128)S(1)}, f32[512,1,128]{0,2,1:T(8,128)}, u32[]{:S(2)}, u32[]{:S(2)}) %collective-permute-start.7) | collective-permute-done | bytes 262176 | tf_op jit(solution)/shard_map/ppermute | solution.py:16
  84.0 1.2 %fusion.20 = bf16[512,128]{0,1:T(8,128)(2,1)S(1)} fusion(f32[512,1,128]{0,2,1:T(8,128)} %collective-permute-done.7, f32[512,1,128]{0,2,1:T(8,128)S(1)} %collective-permute-done.6, bf16[512,128]{0,1:T(8,128)(2,1)S(1)} %get-tuple-element.19, bf16[512,512]{1,0:T(8,128)(2,1)S(1)} %get-tuple-element.23), kind=kOutput, calls=%fused_computation.36 | convolution fusion | flops 67305472 | bytes 1310720 | tf_op jit(solution)/shard_map/hqk,qhd->khd/dot_general | solution.py:40
  85.2 0.8 copy.14
  86.0 6.5 %collective-permute-done.5 = f32[512,1,128]{2,0,1:T(8,128)S(1)} collective-permute-done((f32[512,1,128]{2,0,1:T(8,128)}, f32[512,1,128]{2,0,1:T(8,128)S(1)}, u32[]{:S(2)}, u32[]{:S(2)}) %collective-permute-start.5) | collective-permute-done | bytes 262176 | tf_op jit(solution)/shard_map/ppermute | solution.py:16
  92.5 7.0 %collective-permute-done.4 = f32[512,1,128]{2,0,1:T(8,128)S(1)} collective-permute-done((f32[512,1,128]{2,0,1:T(8,128)S(1)}, f32[512,1,128]{2,0,1:T(8,128)S(1)}, u32[]{:S(2)}, u32[]{:S(2)}) %collective-permute-start.4) | collective-permute-done | bytes 262176 | tf_op jit(solution)/shard_map/ppermute | solution.py:16
  99.5 1.0 %fusion.21 = bf16[512,128]{1,0:T(8,128)(2,1)} fusion(f32[512,1,128]{2,0,1:T(8,128)S(1)} %collective-permute-done.5, f32[512,1,128]{2,0,1:T(8,128)S(1)} %collective-permute-done.4, bf16[512,512]{1,0:T(8,128)(2,1)S(1)} %fusion.8, bf16[512,128]{1,0:T(8,128)(2,1)S(1)} %copy-done), kind=kOutput, calls=%fused_computation.37 | convolution fusion | flops 67371008 | bytes 1310720 | tf_op jit(solution)/shard_map/hqk,qhd->khd/dot_general | solution.py:37
  (53 shorter events, 3.9 us)
Async XLA Ops:
  0.6 17.7 %copy-start = (bf16[512,128]{1,0:T(8,128)(2,1)S(1)}, bf16[512,128]{1,0:T(8,128)(2,1)}, u32[]{:S(2)}) copy-start(bf16[512,128]{1,0:T(8,128)(2,1)} %param.6) | copy-start | bytes 393220
  0.6 21.7 %collective-permute-start = (bf16[512,1,128]{2,0,1:T(8,128)(2,1)}, bf16[512,1,128]{2,0,1:T(8,128)(2,1)S(1)}, u32[]{:S(2)}, u32[]{:S(2)}) collective-permute-start(bf16[512,1,128]{2,0,1:T(8,128)(2,1)} %bitcast.105), channel_id=1, source_target_pairs={{0,8},{8,16},{16,24},{24,32},{32,40},{40,48},{48,56},{56,64},{64,7... | collective-permute-start | bytes 393224 | tf_op jit(solution)/shard_map/ppermute | solution.py:16
  5.5 17.2 %collective-permute-start.2 = (bf16[512,1,128]{2,0,1:T(8,128)(2,1)}, bf16[512,1,128]{2,0,1:T(8,128)(2,1)S(1)}, u32[]{:S(2)}, u32[]{:S(2)}) collective-permute-start(bf16[512,1,128]{2,0,1:T(8,128)(2,1)} %bitcast.106), channel_id=1, source_target_pairs={{0,16},{8,24},{16,32},{24,40},{32,48},{40,56},{48,64},{56,72},{64,... | collective-permute-start | bytes 393224 | tf_op jit(solution)/shard_map/ppermute | solution.py:16
  10.0 16.0 %collective-permute-start.1 = (bf16[512,1,128]{2,0,1:T(8,128)(2,1)}, bf16[512,1,128]{2,0,1:T(8,128)(2,1)}, u32[]{:S(2)}, u32[]{:S(2)}) collective-permute-start(bf16[512,1,128]{2,0,1:T(8,128)(2,1)} %bitcast.107), channel_id=1, source_target_pairs={{0,8},{8,16},{16,24},{24,32},{32,40},{40,48},{48,56},{56,64},{64,7... | collective-permute-start | bytes 393224 | tf_op jit(solution)/shard_map/ppermute | solution.py:16
  13.5 13.8 %collective-permute-start.3 = (bf16[512,1,128]{2,0,1:T(8,128)(2,1)}, bf16[512,1,128]{2,0,1:T(8,128)(2,1)}, u32[]{:S(2)}, u32[]{:S(2)}) collective-permute-start(bf16[512,1,128]{2,0,1:T(8,128)(2,1)} %bitcast.108), channel_id=1, source_target_pairs={{0,16},{8,24},{16,32},{24,40},{32,48},{40,56},{48,64},{56,72},{64,... | collective-permute-start | bytes 393224 | tf_op jit(solution)/shard_map/ppermute | solution.py:16
  18.3 2.9 %copy-start.8 = (bf16[512,128]{1,0:T(8,128)(2,1)S(1)}, bf16[512,128]{1,0:T(8,128)(2,1)}, u32[]{:S(2)}) copy-start(bf16[512,128]{1,0:T(8,128)(2,1)} %param.9) | copy-start | bytes 393220
  20.6 0.7 copy-start.16
  21.3 0.9 copy-start.9
  22.3 1.2 %copy-start.1 = (f32[512,512]{1,0:T(8,128)S(1)}, f32[512,512]{1,0:T(8,128)}, u32[]{:S(2)}) copy-start(f32[512,512]{1,0:T(8,128)} %convolution_multiply_fusion.5) | copy-start | bytes 3145732
  22.3 0.6 copy-start.12
  22.3 0.6 copy-start.14
  22.7 3.0 %copy-start.10 = (bf16[512,1,128]{2,0,1:T(8,128)(2,1)}, bf16[512,1,128]{2,0,1:T(8,128)(2,1)S(1)}, u32[]{:S(2)}) copy-start(bf16[512,1,128]{2,0,1:T(8,128)(2,1)S(1)} %collective-permute-done.2) | copy-start | bytes 393220
  23.5 2.2 %copy-start.6 = (bf16[512,128]{1,0:T(8,128)(2,1)S(1)}, bf16[512,128]{1,0:T(8,128)(2,1)}, u32[]{:S(2)}) copy-start(bf16[512,128]{1,0:T(8,128)(2,1)} %param.8) | copy-start | bytes 393220
  55.3 1.3 %copy-start.2 = (f32[512,512]{1,0:T(8,128)S(1)}, f32[512,512]{1,0:T(8,128)}, u32[]{:S(2)}) copy-start(f32[512,512]{1,0:T(8,128)} %convolution_multiply_fusion.5) | copy-start | bytes 3145732
  56.3 1.0 copy-start.7
  56.3 1.0 copy-start.13
  57.3 5.8 %copy-start.15 = (s32[512]{0:T(512)S(1)}, s32[512]{0:T(512)}, u32[]{:S(2)}) copy-start(s32[512]{0:T(512)} %copy-done.14) | copy-start | bytes 6148
  57.3 5.8 %copy-start.17 = (f32[512,512]{1,0:T(8,128)S(1)}, f32[512,512]{1,0:T(8,128)}, u32[]{:S(2)}) copy-start(f32[512,512]{1,0:T(8,128)} %get-tuple-element.26) | copy-start | bytes 3145732
  57.9 18.1 %collective-permute-start.6 = (f32[512,1,128]{0,2,1:T(8,128)}, f32[512,1,128]{0,2,1:T(8,128)S(1)}, u32[]{:S(2)}, u32[]{:S(2)}) collective-permute-start(f32[512,1,128]{0,2,1:T(8,128)} %convolution_bitcast_fusion.1), channel_id=1, source_target_pairs={{8,0},{16,8},{24,16},{32,24},{40,32},{48,40},{56,48},{64,56},{72,6... | collective-permute-start | bytes 786440 | tf_op jit(solution)/shard_map/ppermute | solution.py:16
  61.2 22.9 %collective-permute-start.7 = (f32[512,1,128]{0,2,1:T(8,128)S(1)}, f32[512,1,128]{0,2,1:T(8,128)}, u32[]{:S(2)}, u32[]{:S(2)}) collective-permute-start(f32[512,1,128]{0,2,1:T(8,128)S(1)} %convolution_bitcast_fusion), channel_id=1, source_target_pairs={{16,0},{24,8},{32,16},{40,24},{48,32},{56,40},{64,48},{72,56},{80,... | collective-permute-start | bytes 786440 | tf_op jit(solution)/shard_map/ppermute | solution.py:16
  65.7 26.8 %collective-permute-start.5 = (f32[512,1,128]{2,0,1:T(8,128)}, f32[512,1,128]{2,0,1:T(8,128)S(1)}, u32[]{:S(2)}, u32[]{:S(2)}) collective-permute-start(f32[512,1,128]{2,0,1:T(8,128)} %fusion.9), channel_id=1, source_target_pairs={{16,0},{24,8},{32,16},{40,24},{48,32},{56,40},{64,48},{72,56},{80,... | collective-permute-start | bytes 786440 | tf_op jit(solution)/shard_map/ppermute | solution.py:16
  69.8 2.4 %copy-start.3 = (bf16[512,128]{1,0:T(8,128)(2,1)S(1)}, bf16[512,128]{1,0:T(8,128)(2,1)}, u32[]{:S(2)}) copy-start(bf16[512,128]{1,0:T(8,128)(2,1)} %param.7) | copy-start | bytes 393220
  70.2 29.3 %collective-permute-start.4 = (f32[512,1,128]{2,0,1:T(8,128)S(1)}, f32[512,1,128]{2,0,1:T(8,128)S(1)}, u32[]{:S(2)}, u32[]{:S(2)}) collective-permute-start(f32[512,1,128]{2,0,1:T(8,128)S(1)} %fusion.10), channel_id=1, source_target_pairs={{8,0},{16,8},{24,16},{32,24},{40,32},{48,40},{56,48},{64,56},{72,6... | collective-permute-start | bytes 786440 | tf_op jit(solution)/shard_map/ppermute | solution.py:16
  72.5 0.9 copy-start.11
  73.4 1.0 copy-start.5
  74.4 0.9 copy-start.4
where the time goes:
time: 101 us
  starting transfers between devices  27.4 us (27%)
  blocking collectives  25.9 us (26%)
  waiting for transfers between devices  21.5 us (21%)
  matrix products  17.4 us (17%)
  local copies, waits for them, and re-layouts  6.37 us (6%)
    ppermute x8, starting transfers between devices, from_behind(): lax.ppermute(value, axis, [(source, source + steps) for source in range(i...  27.4 us
    ppermute x8, waiting for transfers between devices, from_behind(): lax.ppermute(value, axis, [(source, source + steps) for source in range(i...  21.5 us
    psum x1, blocking collectives, local(): lax.psum((jnp.sum(attended, axis=1), jnp.sum(attended * attended, axis=1)...  13.5 us
    psum x1, blocking collectives, local(): lax.psum((jnp.sum(scaled, axis=1), jnp.sum(scaled * normed, axis=1)), 'he...  12.4 us
    unnamed x41, local copies, waits for them, and re-layouts  6.37 us
    dot_general x3, matrix products, silu_parts(): jnp.einsum('qhd,khd->hqk', query_tile, key_tile, preferred_element_type=j...  4.69 us
    dot_general x3, matrix products, tile_backward(): jnp.einsum('qhd,khd->hqk', delta_part, value_part, preferred_element_type...  3.69 us
    dot_general x3, matrix products, local(): jnp.einsum('hqk,khd->qhd', weights, value_part, preferred_element_type=jn...  2.76 us
  transfers between devices with their start and end apart: 8, of which 3 were waited for; matrix products, arithmetic and copies ran while one was open for 16% of the time, Pallas kernels for 0%

commit v1 on v0

v1 whole, which is shorter than its diff:
```python
import functools

import jax
import jax.numpy as jnp
from jax import lax
from jax.experimental import pallas as pl
from jax.experimental.pallas import tpu as pltpu
from jax.sharding import PartitionSpec as P

DH = 128
CH = 128
EPSILON = 1e-05
MESH = pl.DeviceIdType.MESH
F32 = jnp.float32
BF16 = jnp.bfloat16


def dot_nt(a, b):
    return lax.dot_general(a, b, (((1,), (1,)), ((), ())), preferred_element_type=F32)


def dot_nn(a, b):
    return lax.dot_general(a, b, (((1,), (0,)), ((), ())), preferred_element_type=F32)


def kernel(
    rows_n, heads_n, factor,
    bounds_h, q_h, k_h, v_h, g_h, c_h,
    lay_o, gq_o, gk_o, gv_o, gg_o,
    bnd, qb, kb, vb, gb, cb,
    k1, v1, k2, v2, q1, q2, d0, d1, d2,
    srel, erel, fq, ft, pt, att, dk, dv, st_out, st_in,
    lsem, s1, r1, s2, r2, sq, rq, sd, rd, ss, rs,
):
    R = q_h.shape[0]
    NC = R // CH
    features = heads_n * DH
    pos = lax.axis_index("rows")
    head = lax.axis_index("heads")
    right = lax.rem(pos + 1, rows_n)
    right2 = lax.rem(pos + 2, rows_n)
    left = lax.rem(pos + rows_n - 1, rows_n)
    left2 = lax.rem(pos + rows_n - 2, rows_n)
    peers = [lax.rem(head + p, heads_n) for p in range(1, heads_n)]

    def sl(c, n=1):
        return pl.ds(c * CH, n * CH)

    barrier = pltpu.get_barrier_semaphore()
    for who in (left, right, right2):
        pl.semaphore_signal(barrier, inc=1, device_id={"rows": who}, device_id_type=MESH)
    for who in peers:
        pl.semaphore_signal(barrier, inc=1, device_id={"heads": who}, device_id_type=MESH)
    loads = [
        pltpu.make_async_copy(src, dst, lsem.at[n])
        for n, (src, dst) in enumerate(
            ((q_h, qb), (k_h, kb), (v_h, vb), (bounds_h, bnd), (g_h, gb), (c_h, cb))
        )
    ]
    for copy in loads:
        copy.start()
    pl.semaphore_wait(barrier, 3 + len(peers))

    def remote(src, dst, send, recv, **who):
        return pltpu.make_async_remote_copy(
            src_ref=src, dst_ref=dst, send_sem=send, recv_sem=recv,
            device_id=who, device_id_type=MESH,
        )

    kv1, kv2 = {}, {}
    for c in reversed(range(NC)):
        kv1[c] = (
            remote(k_h.at[sl(c)], k1.at[sl(c)], s1.at[0, c], r1.at[0, c], rows=right),
            remote(v_h.at[sl(c)], v1.at[sl(c)], s1.at[1, c], r1.at[1, c], rows=right),
        )
        kv2[c] = (
            remote(k1.at[sl(c)], k2.at[sl(c)], s2.at[0, c], r2.at[0, c], rows=right),
            remote(v1.at[sl(c)], v2.at[sl(c)], s2.at[1, c], r2.at[1, c], rows=right),
        )
        for copy in kv1[c]:
            copy.start()
    q_copies = (
        remote(q_h, q1, sq.at[0], rq.at[0], rows=left),
        remote(q_h, q2, sq.at[1], rq.at[1], rows=left2),
    )
    for copy in q_copies:
        copy.start()
    for copy in loads:
        copy.wait()

    first_row = pos * R
    for c in range(NC):
        for row, dst in ((0, srel), (1, erel)):
            line = bnd[row : row + 1, c * CH : (c + 1) * CH] - first_row
            dst[sl(c), :] = jnp.transpose(jnp.broadcast_to(line, (CH, CH)))

    def parts(raw):
        scores = raw * factor
        sigmoid = 1.0 / (1.0 + jnp.exp(-scores))
        return scores * sigmoid, sigmoid * (1.0 + scores * (1.0 - sigmoid))

    def lanes(n, base):
        return lax.broadcasted_iota(jnp.int32, (CH, n * CH), 1) + base

    def wide(column, n):
        return jnp.concatenate([column] * n, axis=1) if n > 1 else column

    def forward(i, off, kk, vv, lo, hi):
        n = hi - lo
        raw = dot_nt(qb[sl(i), :], kk[sl(lo, n), :])
        at = lanes(n, lo * CH - off * R)
        allowed = at >= wide(srel[sl(i), :], n)
        if off == 0:
            rows = lax.broadcasted_iota(jnp.int32, (CH, n * CH), 0) + i * CH
            allowed = allowed & (at <= rows)
        weights, slope = parts(raw)
        fq[off, sl(i), sl(lo, n)] = jnp.where(allowed, slope, 0.0)
        weights = jnp.where(allowed, weights, 0.0).astype(BF16)
        return dot_nn(weights, vv[sl(lo, n), :])

    def prepare(j, off, qq, lo, hi):
        n = hi - lo
        raw = dot_nt(kb[sl(j), :], qq[sl(lo, n), :])
        at = lanes(n, lo * CH + off * R)
        allowed = at <= wide(erel[sl(j), :], n)
        if off == 0:
            keys = lax.broadcasted_iota(jnp.int32, (CH, n * CH), 0) + j * CH
            allowed = allowed & (at >= keys)
        weights, slope = parts(raw)
        ft[off, sl(j), sl(lo, n)] = jnp.where(allowed, slope, 0.0)
        pt[off, sl(j), sl(lo, n)] = jnp.where(allowed, weights, 0.0).astype(BF16)

    for i in range(NC):
        att[sl(i), :] = forward(i, 0, kb, vb, 0, i + 1)
    for j in range(NC):
        prepare(j, 0, qb, j, NC)
    q_copies[0].wait_recv()
    for j in range(NC):
        prepare(j, 1, q1, 0, NC)
    for c in reversed(range(NC)):
        for copy in kv1[c]:
            copy.wait_recv()
        for copy in kv2[c]:
            copy.start()
    for i in range(NC):
        att[sl(i), :] += forward(i, 1, k1, v1, 0, NC)
    q_copies[1].wait_recv()
    for j in range(NC):
        prepare(j, 2, q2, 0, j + 1)

    def stats_copies(c):
        return [
            remote(
                st_out.at[c], st_in.at[head, c], ss.at[p, c], rs.at[head, c], heads=who
            )
            for p, who in enumerate(peers)
        ]

    def stats_send(i):
        rows_t = jnp.transpose(att[sl(i), :])
        scaled_t = jnp.transpose(cb[sl(i), :].astype(F32) * gb[sl(i), :].astype(F32))
        for n, term in enumerate((rows_t, rows_t * rows_t, scaled_t, scaled_t * rows_t)):
            st_out[i, n : n + 1, :] = jnp.sum(term, axis=0, keepdims=True)
        st_in[head, i, 0:4, :] = st_out[i, 0:4, :]
        for copy in stats_copies(i):
            copy.start()

    def stats_use(i):
        for who in peers:
            pltpu.make_async_remote_copy(
                src_ref=st_out.at[i], dst_ref=st_in.at[who, i], send_sem=ss.at[0, i],
                recv_sem=rs.at[who, i], device_id={"heads": who}, device_id_type=MESH,
            ).wait_recv()
        total = st_in[0, i, 0:4, :]
        for p in range(1, heads_n):
            total = total + st_in[p, i, 0:4, :]
        average = total[0:1] / features
        inverse = lax.rsqrt(total[1:2] / features - average * average + EPSILON)
        grad_mean = total[2:3] / features
        cross_mean = inverse * (total[3:4] - average * total[2:3]) / features

        def column(line):
            return jnp.transpose(jnp.broadcast_to(line, (CH, CH)))

        inverse_c = column(inverse)
        normed = (att[sl(i), :] - column(average)) * inverse_c
        gate = gb[sl(i), :].astype(F32)
        upstream = cb[sl(i), :].astype(F32)
        delta = inverse_c * (
            upstream * gate - column(grad_mean) - normed * column(cross_mean)
        )
        d0[sl(i), :] = delta.astype(BF16)
        lay_o[sl(i), :] = (normed * gate).astype(BF16)
        gg_o[sl(i), :] = (upstream * normed).astype(BF16)
        for copy in delta_copies[i]:
            copy.start()

    delta_copies = {
        c: (
            remote(d0.at[sl(c)], d1.at[sl(c)], sd.at[0, c], rd.at[0, c], rows=left),
            remote(d0.at[sl(c)], d2.at[sl(c)], sd.at[1, c], rd.at[1, c], rows=left2),
        )
        for c in range(NC)
    }

    def query_grad(i):
        total = None
        for off, kk, vv, lo, hi in (
            (0, kb, vb, 0, i + 1), (1, k1, v1, 0, NC), (2, k2, v2, i, NC)
        ):
            n = hi - lo
            pulled = dot_nt(d0[sl(i), :], vv[sl(lo, n), :])
            grad = (pulled * fq[off, sl(i), sl(lo, n)]).astype(BF16)
            term = dot_nn(grad, kk[sl(lo, n), :])
            total = term if total is None else total + term
        gq_o[sl(i), :] = (total * factor).astype(BF16)

    def key_grad(i, off, qq, dd, lo, hi, fresh=False):
        n = hi - lo
        delta = dd[sl(i), :]
        pulled = dot_nt(vb[sl(lo, n), :], delta)
        grad = (pulled * ft[off, sl(lo, n), sl(i)]).astype(BF16)
        key_add = dot_nn(grad, qq[sl(i), :])
        value_add = dot_nn(pt[off, sl(lo, n), sl(i)], delta)
        if fresh:
            dk[sl(lo, n), :] = key_add
            dv[sl(lo, n), :] = value_add
        else:
            dk[sl(lo, n), :] += key_add
            dv[sl(lo, n), :] += value_add

    def local_grads(i):
        query_grad(i)
        key_grad(i, 0, qb, d0, 0, i + 1, fresh=i == NC - 1)

    def remote_grads(i):
        delta_copies[i][0].wait_recv()
        key_grad(i, 1, q1, d1, 0, NC)
        delta_copies[i][1].wait_recv()
        key_grad(i, 2, q2, d2, i, NC)

    for c in reversed(range(NC)):
        for copy in kv2[c]:
            copy.wait_recv()
        for i in range(c + 1):
            att[sl(i), :] += forward(i, 2, k2, v2, c, c + 1)
        stats_send(c)
        if c + 1 < NC:
            stats_use(c + 1)
        if c + 2 < NC:
            local_grads(c + 2)
    local_grads(1)
    for i in (3, 2):
        remote_grads(i)
    stats_use(0)
    local_grads(0)
    for i in (1, 0):
        remote_grads(i)
    gk_o[...] = (dk[...] * factor).astype(BF16)
    gv_o[...] = dv[...].astype(BF16)

    for c in range(NC):
        for copy in (*kv1[c], *kv2[c], *delta_copies[c], *stats_copies(c)):
            copy.wait_send()
    for copy in q_copies:
        copy.wait_send()


def local(rows_n, heads_n, queries, key_vectors, value_vectors, gating, bounds, cotangent):
    R, width = queries.shape
    NC = R // CH
    block = (R, width)
    bf = lambda *shape: pltpu.VMEM(shape, BF16)
    fl = lambda *shape: pltpu.VMEM(shape, F32)
    dma = lambda *shape: pltpu.SemaphoreType.DMA(shape)
    out = jax.ShapeDtypeStruct(block, BF16)
    return pl.pallas_call(
        functools.partial(kernel, rows_n, heads_n, DH ** (-0.5)),
        out_shape=(out,) * 5,
        in_specs=[pl.BlockSpec(memory_space=pl.ANY)] * 6,
        out_specs=(pl.BlockSpec(memory_space=pltpu.VMEM),) * 5,
        scratch_shapes=[
            pltpu.VMEM((2, R), jnp.int32),
            *[bf(*block)] * 5,
            *[bf(*block)] * 9,
            pltpu.VMEM((R, CH), jnp.int32), pltpu.VMEM((R, CH), jnp.int32),
            fl(3, R, R), fl(3, R, R), bf(3, R, R),
            fl(*block), fl(*block), fl(*block),
            fl(NC, 8, CH), fl(heads_n, NC, 8, CH),
            dma(6), dma(2, NC), dma(2, NC), dma(2, NC), dma(2, NC),
            dma(2), dma(2), dma(2, NC), dma(2, NC),
            dma(heads_n - 1, NC), dma(heads_n, NC),
        ],
        compiler_params=pltpu.CompilerParams(collective_id=0, has_side_effects=True),
        name="jagged_attention",
    )(bounds, queries, key_vectors, value_vectors, gating, cotangent)


def solution(mesh):
    spec = P("rows", "heads")
    return jax.shard_map(
        functools.partial(local, mesh.shape["rows"], mesh.shape["heads"]),
        mesh=mesh,
        in_specs=(spec, spec, spec, spec, P(None, "rows"), spec),
        out_specs=(spec,) * 5,
        check_vma=False,
    )
```

time: 101 us -> 55.2 us (0.55)
  the two profiles are of different devices: /device:TPU:248 before, /device:TPU:1 now
where the time goes in v1:
time: 55.2 us; the launch traced here: 55 us
  Pallas kernels  49.2 us (89%)
  local copies, waits for them, and re-layouts  5.11 us (9%)
  between operations  0.66 us (1%)
    pallas_call x1, Pallas kernels, local(): pl.pallas_call(functools.partial(kernel, rows_n, heads_n, DH ** (-0.5)),...  49.2 us
    unnamed x13, local copies, waits for them, and re-layouts  5.11 us

profile of v1, /device:TPU:1, one launch (start us, length us, event | category | flops | bytes accessed | tf_op | source)
XLA Modules:
  0.0 55.0 jit_solution(17193242223225868808)
XLA Ops:
  0.6 49.2 %jagged_attention.1 = (bf16[512,128]{1,0:T(8,128)(2,1)}, bf16[512,128]{1,0:T(8,128)(2,1)}, bf16[512,128]{1,0:T(8,128)(2,1)}, bf16[512,128]{1,0:T(8,128)(2,1)}, bf16[512,128]{1,0:T(8,128)(2,1)}) custom-call(s32[2,512]{1,0:T(2,128)} %bounds_h.1, bf16[512,128]{1,0:T(8,128)(2,1)} %q_h.1, bf16[512,128]{1,0:T(8,128)(2,1)} %k_h.1, bf16[512,128]{1,0:T(8,128)(2,1)} %v_h.1, ...), custom_call_target="tpu_custom_call" | custom-call | tf_op jit(solution)/shard_map/jagged_attention/pallas_call | solution.py:277
  49.9 0.0 copy-start.3
  49.9 1.6 %copy.16 = bf16[512,128]{1,0:T(8,128)(2,1)} copy(bf16[512,128]{1,0:T(8,128)(2,1)} %get-tuple-element.10) | data formatting | bytes 262144
  51.5 0.0 copy-done.3
  51.5 0.0 copy-start.2
  51.5 0.7 %copy.17 = bf16[512,128]{1,0:T(8,128)(2,1)} copy(bf16[512,128]{1,0:T(8,128)(2,1)S(1)} %copy-done.3) | data formatting | bytes 262144
  52.2 0.3 copy-done.2
  52.5 0.0 copy-start.1
  52.5 0.7 %copy.18 = bf16[512,128]{1,0:T(8,128)(2,1)} copy(bf16[512,128]{1,0:T(8,128)(2,1)S(1)} %copy-done.2) | data formatting | bytes 262144
  53.1 0.3 copy-done.1
  53.4 0.0 copy-start
  53.4 0.7 %copy.19 = bf16[512,128]{1,0:T(8,128)(2,1)} copy(bf16[512,128]{1,0:T(8,128)(2,1)S(1)} %copy-done.1) | data formatting | bytes 262144
  54.1 0.3 copy-done
  54.4 0.7 %copy.20 = bf16[512,128]{1,0:T(8,128)(2,1)} copy(bf16[512,128]{1,0:T(8,128)(2,1)S(1)} %copy-done) | data formatting | bytes 262144
Async XLA Ops:
  49.9 1.6 %copy-start.3 = (bf16[512,128]{1,0:T(8,128)(2,1)S(1)}, bf16[512,128]{1,0:T(8,128)(2,1)}, u32[]{:S(2)}) copy-start(bf16[512,128]{1,0:T(8,128)(2,1)} %get-tuple-element.11) | copy-start | bytes 393220
  51.5 1.0 %copy-start.2 = (bf16[512,128]{1,0:T(8,128)(2,1)S(1)}, bf16[512,128]{1,0:T(8,128)(2,1)}, u32[]{:S(2)}) copy-start(bf16[512,128]{1,0:T(8,128)(2,1)} %get-tuple-element.12) | copy-start | bytes 393220
  52.5 1.0 %copy-start.1 = (bf16[512,128]{1,0:T(8,128)(2,1)S(1)}, bf16[512,128]{1,0:T(8,128)(2,1)}, u32[]{:S(2)}) copy-start(bf16[512,128]{1,0:T(8,128)(2,1)} %get-tuple-element.13) | copy-start | bytes 393220
  53.4 1.0 %copy-start = (bf16[512,128]{1,0:T(8,128)(2,1)S(1)}, bf16[512,128]{1,0:T(8,128)(2,1)}, u32[]{:S(2)}) copy-start(bf16[512,128]{1,0:T(8,128)(2,1)} %get-tuple-element.14) | copy-start | bytes 393220

commit v2 on v1

v2 whole, which is shorter than its diff:
```python
import functools

import jax
import jax.numpy as jnp
from jax import lax
from jax.experimental import pallas as pl
from jax.experimental.pallas import tpu as pltpu
from jax.sharding import PartitionSpec as P

DH = 128
CH = 128
EPSILON = 1e-05
MESH = pl.DeviceIdType.MESH
F32 = jnp.float32
BF16 = jnp.bfloat16


def dot_nt(a, b):
    return lax.dot_general(a, b, (((1,), (1,)), ((), ())), preferred_element_type=F32)


def dot_nn(a, b):
    return lax.dot_general(a, b, (((1,), (0,)), ((), ())), preferred_element_type=F32)


def kernel(
    rows_n, heads_n, factor,
    bounds_h, q_h, k_h, v_h, g_h, c_h,
    lay_o, gq_o, gk_o, gv_o, gg_o,
    bnd, qb, kb, vb, gb, cb,
    k1, v1, k2, v2, q1, q2, d0, d1, d2,
    srel, erel, fq, ft, pt, att, dk, dv, st_out, st_in,
    lsem, s1, r1, s2, r2, sq, rq, sd, rd, ss, rs,
):
    R = q_h.shape[0]
    NC = R // CH
    features = heads_n * DH
    pos = lax.axis_index("rows")
    head = lax.axis_index("heads")
    right = lax.rem(pos + 1, rows_n)
    right2 = lax.rem(pos + 2, rows_n)
    left = lax.rem(pos + rows_n - 1, rows_n)
    left2 = lax.rem(pos + rows_n - 2, rows_n)
    has_left, has_left2 = pos >= 1, pos >= 2
    has_right, has_right2 = pos < rows_n - 1, pos < rows_n - 2
    peers = [lax.rem(head + p, heads_n) for p in range(1, heads_n)]

    def sl(c, n=1):
        return pl.ds(c * CH, n * CH)

    barrier = pltpu.get_barrier_semaphore()
    for there, who in ((has_left, left), (has_right, right), (has_right2, right2)):
        @pl.when(there)
        def _():
            pl.semaphore_signal(barrier, inc=1, device_id={"rows": who}, device_id_type=MESH)
    for who in peers:
        pl.semaphore_signal(barrier, inc=1, device_id={"heads": who}, device_id_type=MESH)
    loads = [
        pltpu.make_async_copy(src, dst, lsem.at[n])
        for n, (src, dst) in enumerate(
            ((q_h, qb), (k_h, kb), (v_h, vb), (bounds_h, bnd), (g_h, gb), (c_h, cb))
        )
    ]
    for copy in loads:
        copy.start()
    greeters = sum(there.astype(jnp.int32) for there in (has_left, has_left2, has_right))
    pl.semaphore_wait(barrier, greeters + len(peers))

    def remote(src, dst, send, recv, **who):
        return pltpu.make_async_remote_copy(
            src_ref=src, dst_ref=dst, send_sem=send, recv_sem=recv,
            device_id=who, device_id_type=MESH,
        )

    kv1, kv2, delta_copies = {}, {}, {}
    for c in range(NC):
        kv1[c] = (
            remote(k_h.at[sl(c)], k1.at[sl(c)], s1.at[0, c], r1.at[0, c], rows=right),
            remote(v_h.at[sl(c)], v1.at[sl(c)], s1.at[1, c], r1.at[1, c], rows=right),
        )
        kv2[c] = (
            remote(k1.at[sl(c)], k2.at[sl(c)], s2.at[0, c], r2.at[0, c], rows=right),
            remote(v1.at[sl(c)], v2.at[sl(c)], s2.at[1, c], r2.at[1, c], rows=right),
        )
        delta_copies[c] = (
            remote(d0.at[sl(c)], d1.at[sl(c)], sd.at[0, c], rd.at[0, c], rows=left),
            remote(d0.at[sl(c)], d2.at[sl(c)], sd.at[1, c], rd.at[1, c], rows=left2),
        )
    q_copies = (
        remote(q_h, q1, sq.at[0], rq.at[0], rows=left),
        remote(q_h, q2, sq.at[1], rq.at[1], rows=left2),
    )

    @pl.when(has_right)
    def _():
        for c in reversed(range(NC)):
            for copy in kv1[c]:
                copy.start()

    @pl.when(has_left)
    def _():
        q_copies[0].start()

    @pl.when(has_left2)
    def _():
        q_copies[1].start()

    for copy in loads:
        copy.wait()

    first_row = pos * R
    for c in range(NC):
        for row, dst in ((0, srel), (1, erel)):
            line = bnd[row : row + 1, c * CH : (c + 1) * CH] - first_row
            dst[sl(c), :] = jnp.transpose(jnp.broadcast_to(line, (CH, CH)))

    def parts(raw):
        scores = raw * factor
        sigmoid = 1.0 / (1.0 + jnp.exp(-scores))
        return scores * sigmoid, sigmoid * (1.0 + scores * (1.0 - sigmoid))

    def lanes(n, base):
        return lax.broadcasted_iota(jnp.int32, (n * CH, CH), 1) + base

    def sublanes(n, base):
        return lax.broadcasted_iota(jnp.int32, (n * CH, CH), 0) + base

    def forward(c, off, kk, vv, lo, hi, fresh=False):
        n = hi - lo
        raw = dot_nt(qb[sl(lo, n), :], kk[sl(c), :])
        at = lanes(n, c * CH - off * R)
        allowed = at >= srel[sl(lo, n), :]
        if off == 0:
            allowed = allowed & (at <= sublanes(n, lo * CH))
        weights, slope = parts(raw)
        fq[off, c, sl(lo, n), :] = jnp.where(allowed, slope, 0.0)
        weights = jnp.where(allowed, weights, 0.0).astype(BF16)
        term = dot_nn(weights, vv[sl(c), :])
        if fresh:
            att[sl(lo, n), :] = term
        else:
            att[sl(lo, n), :] += term

    def prepare(i, off, qq, lo, hi):
        n = hi - lo
        raw = dot_nt(kb[sl(lo, n), :], qq[sl(i), :])
        at = lanes(n, i * CH + off * R)
        allowed = at <= erel[sl(lo, n), :]
        if off == 0:
            allowed = allowed & (at >= sublanes(n, lo * CH))
        weights, slope = parts(raw)
        ft[off, i, sl(lo, n), :] = jnp.where(allowed, slope, 0.0)
        pt[off, i, sl(lo, n), :] = jnp.where(allowed, weights, 0.0).astype(BF16)

    def stats_copies(c):
        return [
            remote(
                st_out.at[c], st_in.at[head, c], ss.at[p, c], rs.at[head, c], heads=who
            )
            for p, who in enumerate(peers)
        ]

    def stats_send(i):
        rows_t = jnp.transpose(att[sl(i), :])
        scaled_t = jnp.transpose(cb[sl(i), :].astype(F32) * gb[sl(i), :].astype(F32))
        for n, term in enumerate((rows_t, rows_t * rows_t, scaled_t, scaled_t * rows_t)):
            st_out[i, n : n + 1, :] = jnp.sum(term, axis=0, keepdims=True)
        st_in[head, i, 0:4, :] = st_out[i, 0:4, :]
        for copy in stats_copies(i):
            copy.start()

    def stats_use(i):
        for who in peers:
            remote(
                st_out.at[i], st_in.at[who, i], ss.at[0, i], rs.at[who, i], heads=who
            ).wait_recv()
        total = st_in[0, i, 0:4, :]
        for p in range(1, heads_n):
            total = total + st_in[p, i, 0:4, :]
        average = total[0:1] / features
        inverse = lax.rsqrt(total[1:2] / features - average * average + EPSILON)
        grad_mean = total[2:3] / features
        cross_mean = inverse * (total[3:4] - average * total[2:3]) / features

        def column(line):
            return jnp.transpose(jnp.broadcast_to(line, (CH, CH)))

        inverse_c = column(inverse)
        normed = (att[sl(i), :] - column(average)) * inverse_c
        gate = gb[sl(i), :].astype(F32)
        upstream = cb[sl(i), :].astype(F32)
        delta = inverse_c * (
            upstream * gate - column(grad_mean) - normed * column(cross_mean)
        )
        d0[sl(i), :] = delta.astype(BF16)
        lay_o[sl(i), :] = (normed * gate).astype(BF16)
        gg_o[sl(i), :] = (upstream * normed).astype(BF16)

        @pl.when(has_left)
        def _():
            delta_copies[i][0].start()

        @pl.when(has_left2)
        def _():
            delta_copies[i][1].start()

    def query_grad(c, off, kk, vv, lo, hi, fresh=False):
        n = hi - lo
        pulled = dot_nt(d0[sl(lo, n), :], vv[sl(c), :])
        grad = (pulled * fq[off, c, sl(lo, n), :]).astype(BF16)
        term = dot_nn(grad, kk[sl(c), :])
        if fresh:
            att[sl(lo, n), :] = term
        else:
            att[sl(lo, n), :] += term

    def query_grads(lo, hi):
        for c in range(hi):
            query_grad(c, 0, kb, vb, max(lo, c), hi, fresh=c == 0)

        @pl.when(has_left)
        def _():
            for c in range(NC):
                query_grad(c, 1, k1, v1, lo, hi)

        @pl.when(has_left2)
        def _():
            for c in range(lo, NC):
                query_grad(c, 2, k2, v2, lo, min(hi, c + 1))

        gq_o[sl(lo, hi - lo), :] = (att[sl(lo, hi - lo), :] * factor).astype(BF16)

    def key_grad(i, off, qq, dd, lo, hi, fresh=False):
        n = hi - lo
        delta = dd[sl(i), :]
        pulled = dot_nt(vb[sl(lo, n), :], delta)
        grad = (pulled * ft[off, i, sl(lo, n), :]).astype(BF16)
        key_add = dot_nn(grad, qq[sl(i), :])
        value_add = dot_nn(pt[off, i, sl(lo, n), :], delta)
        if fresh:
            dk[sl(lo, n), :] = key_add
            dv[sl(lo, n), :] = value_add
        else:
            dk[sl(lo, n), :] += key_add
            dv[sl(lo, n), :] += value_add

    def remote_grads(i):
        @pl.when(has_right)
        def _():
            delta_copies[i][0].wait_recv()
            key_grad(i, 1, q1, d1, 0, NC)

        @pl.when(has_right2)
        def _():
            delta_copies[i][1].wait_recv()
            key_grad(i, 2, q2, d2, i, NC)

    for c in range(NC):
        forward(c, 0, kb, vb, c, NC, fresh=c == 0)
    for i in range(NC):
        prepare(i, 0, qb, 0, i + 1)
    for c in reversed(range(NC)):
        @pl.when(has_left)
        def _():
            for copy in kv1[c]:
                copy.wait_recv()

            @pl.when(has_right)
            def _():
                for copy in kv2[c]:
                    copy.start()

            forward(c, 1, k1, v1, 0, NC)

    @pl.when(has_right)
    def _():
        q_copies[0].wait_recv()
        for i in range(NC):
            prepare(i, 1, q1, 0, NC)

    @pl.when(has_right2)
    def _():
        q_copies[1].wait_recv()
        for i in range(NC):
            prepare(i, 2, q2, i, NC)

    for c in reversed(range(NC)):
        @pl.when(has_left2)
        def _():
            for copy in kv2[c]:
                copy.wait_recv()
            forward(c, 2, k2, v2, 0, c + 1)

        stats_send(c)
        if c + 1 < NC:
            stats_use(c + 1)
            key_grad(c + 1, 0, qb, d0, 0, c + 2, fresh=c + 1 == NC - 1)
    query_grads(NC // 2, NC)
    for i in reversed(range(NC // 2, NC)):
        remote_grads(i)
    stats_use(0)
    key_grad(0, 0, qb, d0, 0, 1)
    query_grads(0, NC // 2)
    for i in reversed(range(NC // 2)):
        remote_grads(i)
    gk_o[...] = (dk[...] * factor).astype(BF16)
    gv_o[...] = dv[...].astype(BF16)

    @pl.when(has_right)
    def _():
        for c in range(NC):
            for copy in kv1[c]:
                copy.wait_send()

    @pl.when(has_left & has_right)
    def _():
        for c in range(NC):
            for copy in kv2[c]:
                copy.wait_send()

    for n, there in enumerate((has_left, has_left2)):
        @pl.when(there)
        def _():
            q_copies[n].wait_send()
            for c in range(NC):
                delta_copies[c][n].wait_send()

    for c in range(NC):
        for copy in stats_copies(c):
            copy.wait_send()


def store_kernel(*refs):
    sources, results, sems = refs[:5], refs[5:10], refs[10]
    copies = [
        pltpu.make_async_copy(src, dst, sems.at[n])
        for n, (src, dst) in enumerate(zip(sources, results))
    ]
    for copy in copies:
        copy.start()
    for copy in copies:
        copy.wait()


def local(rows_n, heads_n, queries, key_vectors, value_vectors, gating, bounds, cotangent):
    R, width = queries.shape
    NC = R // CH
    block = (R, width)
    bf = lambda *shape: pltpu.VMEM(shape, BF16)
    fl = lambda *shape: pltpu.VMEM(shape, F32)
    dma = lambda *shape: pltpu.SemaphoreType.DMA(shape)
    out = jax.ShapeDtypeStruct(block, BF16)
    held = pl.pallas_call(
        functools.partial(kernel, rows_n, heads_n, DH ** (-0.5)),
        out_shape=(pltpu.VMEM(block, BF16),) * 5,
        in_specs=[pl.BlockSpec(memory_space=pl.ANY)] * 6,
        out_specs=(pl.BlockSpec(memory_space=pltpu.VMEM),) * 5,
        scratch_shapes=[
            pltpu.VMEM((2, R), jnp.int32),
            *[bf(*block)] * 5,
            *[bf(*block)] * 9,
            pltpu.VMEM((R, CH), jnp.int32), pltpu.VMEM((R, CH), jnp.int32),
            fl(3, NC, R, CH), fl(3, NC, R, CH), bf(3, NC, R, CH),
            fl(*block), fl(*block), fl(*block),
            fl(NC, 8, CH), fl(heads_n, NC, 8, CH),
            dma(6), dma(2, NC), dma(2, NC), dma(2, NC), dma(2, NC),
            dma(2), dma(2), dma(2, NC), dma(2, NC),
            dma(heads_n - 1, NC), dma(heads_n, NC),
        ],
        compiler_params=pltpu.CompilerParams(collective_id=0, has_side_effects=True),
        name="jagged_attention",
    )(bounds, queries, key_vectors, value_vectors, gating, cotangent)
    return pl.pallas_call(
        store_kernel,
        out_shape=(out,) * 5,
        in_specs=[pl.BlockSpec(memory_space=pltpu.VMEM)] * 5,
        out_specs=(pl.BlockSpec(memory_space=pl.ANY),) * 5,
        scratch_shapes=[dma(5)],
        name="store_outputs",
    )(*[pltpu.with_memory_space_constraint(x, pltpu.VMEM) for x in held])


def solution(mesh):
    spec = P("rows", "heads")
    return jax.shard_map(
        functools.partial(local, mesh.shape["rows"], mesh.shape["heads"]),
        mesh=mesh,
        in_specs=(spec, spec, spec, spec, P(None, "rows"), spec),
        out_specs=(spec,) * 5,
        check_vma=False,
    )
```

time: 55.2 us -> 38.6 us (0.70)
  Pallas kernels: 49.2 us -> 37.8 us
  local copies, waits for them, and re-layouts: 5.11 us -> 0 us
    pallas_call x1, Pallas kernels: 49.2 us -> 37 us  [local(): pl.pallas_call(functools.partial(kernel, rows_n, heads_n, DH ** (-0.5)),...]
    unnamed x13 -> x0, local copies, waits for them, and re-layouts: 5.11 us -> none
    pallas_call x0 -> x1, Pallas kernels: none -> 0.87 us  [local(): pl.pallas_call(store_kernel, out_shape=(out,) * 5, in_specs=[pl.BlockSpec...]
where the time goes in v2:
time: 38.6 us; the launch traced here: 38.5 us
  Pallas kernels  37.8 us (98%)
  between operations  0.64 us (2%)
    pallas_call x1, Pallas kernels, local(): pl.pallas_call(functools.partial(kernel, rows_n, heads_n, DH ** (-0.5)),...  37 us
    pallas_call x1, Pallas kernels, local(): pl.pallas_call(store_kernel, out_shape=(out,) * 5, in_specs=[pl.BlockSpec...  0.87 us

profile of v2, /device:TPU:1, one launch (start us, length us, event | category | flops | bytes accessed | tf_op | source)
XLA Modules:
  0.0 38.5 jit_solution(1620006146129151001)
XLA Ops:
  0.6 37.0 %jagged_attention.1 = (bf16[512,128]{1,0:T(8,128)(2,1)S(1)}, bf16[512,128]{1,0:T(8,128)(2,1)S(1)}, bf16[512,128]{1,0:T(8,128)(2,1)S(1)}, bf16[512,128]{1,0:T(8,128)(2,1)S(1)}, bf16[512,128]{1,0:T(8,128)(2,1)S(1)}) custom-call(s32[2,512]{1,0:T(2,128)} %bounds_h.1, bf16[512,128]{1,0:T(8,128)(2,1)} %q_h.1, bf16[512,128]{1,0:T(8,128)(2,1)} %k_h.1, ...), custom_call_target="tpu_custom_call" | custom-call | tf_op jit(solution)/shard_map/jagged_attention/pallas_call | solution.py:353
  37.6 0.9 %store_outputs.1 = (bf16[512,128]{1,0:T(8,128)(2,1)}, bf16[512,128]{1,0:T(8,128)(2,1)}, bf16[512,128]{1,0:T(8,128)(2,1)}, bf16[512,128]{1,0:T(8,128)(2,1)}, bf16[512,128]{1,0:T(8,128)(2,1)}) custom-call(bf16[512,128]{1,0:T(8,128)(2,1)S(1)} %get-tuple-element.10.refs_0_, bf16[512,128]{1,0:T(8,128)(2,1)S(1)} %get-tuple-element.11.refs_1_, ...), custom_call_target="tpu_custom_call" | custom-call | tf_op jit(solution)/shard_map/store_outputs/pallas_call | solution.py:373

commit v3 on v2

--- a/solution.py
+++ b/solution.py
@@ -9,6 +9,8 @@
 
 DH = 128
 CH = 128
+LOG2E = 1.4426950408889634
+MASKED = -1e30
 EPSILON = 1e-05
 MESH = pl.DeviceIdType.MESH
 F32 = jnp.float32
@@ -28,9 +30,9 @@
     bounds_h, q_h, k_h, v_h, g_h, c_h,
     lay_o, gq_o, gk_o, gv_o, gg_o,
     bnd, qb, kb, vb, gb, cb,
-    k1, v1, k2, v2, q1, q2, d0, d1, d2,
+    k1, v1, k2, v2, q1, q2, d0, d1, d2, far, o_out, o_in,
     srel, erel, fq, ft, pt, att, dk, dv, st_out, st_in,
-    lsem, s1, r1, s2, r2, sq, rq, sd, rd, ss, rs,
+    lsem, s1, r1, s2, r2, so, ro, sq, rq, sd, rd, ss, rs,
 ):
     R = q_h.shape[0]
     NC = R // CH
@@ -38,9 +40,7 @@
     pos = lax.axis_index("rows")
     head = lax.axis_index("heads")
     right = lax.rem(pos + 1, rows_n)
-    right2 = lax.rem(pos + 2, rows_n)
     left = lax.rem(pos + rows_n - 1, rows_n)
-    left2 = lax.rem(pos + rows_n - 2, rows_n)
     has_left, has_left2 = pos >= 1, pos >= 2
     has_right, has_right2 = pos < rows_n - 1, pos < rows_n - 2
     peers = [lax.rem(head + p, heads_n) for p in range(1, heads_n)]
@@ -49,7 +49,7 @@
         return pl.ds(c * CH, n * CH)
 
     barrier = pltpu.get_barrier_semaphore()
-    for there, who in ((has_left, left), (has_right, right), (has_right2, right2)):
+    for there, who in ((has_left, left), (has_right, right)):
         @pl.when(there)
         def _():
             pl.semaphore_signal(barrier, inc=1, device_id={"rows": who}, device_id_type=MESH)
@@ -63,7 +63,7 @@
     ]
     for copy in loads:
         copy.start()
-    greeters = sum(there.astype(jnp.int32) for there in (has_left, has_left2, has_right))
+    greeters = has_left.astype(jnp.int32) + has_right.astype(jnp.int32)
     pl.semaphore_wait(barrier, greeters + len(peers))
 
     def remote(src, dst, send, recv, **who):
@@ -84,11 +84,15 @@
         )
         delta_copies[c] = (
             remote(d0.at[sl(c)], d1.at[sl(c)], sd.at[0, c], rd.at[0, c], rows=left),
-            remote(d0.at[sl(c)], d2.at[sl(c)], sd.at[1, c], rd.at[1, c], rows=left2),
-        )
+            remote(d1.at[sl(c)], d2.at[sl(c)], sd.at[1, c], rd.at[1, c], rows=left),
+        )
+    o_copies = [
+        remote(o_out.at[sl(c)], o_in.at[sl(c)], so.at[c], ro.at[c], rows=right)
+        for c in range(NC)
+    ]
     q_copies = (
         remote(q_h, q1, sq.at[0], rq.at[0], rows=left),
-        remote(q_h, q2, sq.at[1], rq.at[1], rows=left2),
+        remote(q1, q2, sq.at[1], rq.at[1], rows=left),
     )
 
     @pl.when(has_right)
@@ -100,10 +104,6 @@
     @pl.when(has_left)
     def _():
         q_copies[0].start()
-
-    @pl.when(has_left2)
-    def _():
-        q_copies[1].start()
 
     for copy in loads:
         copy.wait()
@@ -114,10 +114,12 @@
             line = bnd[row : row + 1, c * CH : (c + 1) * CH] - first_row
             dst[sl(c), :] = jnp.transpose(jnp.broadcast_to(line, (CH, CH)))
 
-    def parts(raw):
+    def parts(raw, allowed):
+        raw = jnp.where(allowed, raw, MASKED)
         scores = raw * factor
-        sigmoid = 1.0 / (1.0 + jnp.exp(-scores))
-        return scores * sigmoid, sigmoid * (1.0 + scores * (1.0 - sigmoid))
+        sigmoid = 1.0 / (1.0 + jnp.exp2(raw * (-factor * LOG2E)))
+        weights = scores * sigmoid
+        return weights, sigmoid * ((1.0 + scores) - weights)
 
     def lanes(n, base):
         return lax.broadcasted_iota(jnp.int32, (n * CH, CH), 1) + base
@@ -125,32 +127,59 @@
     def sublanes(n, base):
         return lax.broadcasted_iota(jnp.int32, (n * CH, CH), 0) + base
 
-    def forward(c, off, kk, vv, lo, hi, fresh=False):
+    def halves(value, w):
+        return [value[:, m * CH : (m + 1) * CH] for m in range(w)]
+
+    def joined(values):
+        return values[0] if len(values) == 1 else jnp.concatenate(values, axis=1)
+
+    def forward(c, w, off, kk, vv, lo, hi, fresh=False):
         n = hi - lo
-        raw = dot_nt(qb[sl(lo, n), :], kk[sl(c), :])
-        at = lanes(n, c * CH - off * R)
-        allowed = at >= srel[sl(lo, n), :]
-        if off == 0:
-            allowed = allowed & (at <= sublanes(n, lo * CH))
-        weights, slope = parts(raw)
-        fq[off, c, sl(lo, n), :] = jnp.where(allowed, slope, 0.0)
-        weights = jnp.where(allowed, weights, 0.0).astype(BF16)
-        term = dot_nn(weights, vv[sl(c), :])
+        packed = []
+        for m, raw in enumerate(halves(dot_nt(qb[sl(lo, n), :], kk[sl(c, w), :]), w)):
+            at = lanes(n, (c + m) * CH - off * R)
+            allowed = at >= srel[sl(lo, n), :]
+            if off == 0:
+                allowed = allowed & (at <= sublanes(n, lo * CH))
+            weights, slope = parts(raw, allowed)
+            fq[off, c + m, sl(lo, n), :] = slope
+            packed.append(weights.astype(BF16))
+        term = dot_nn(joined(packed), vv[sl(c, w), :])
         if fresh:
             att[sl(lo, n), :] = term
         else:
             att[sl(lo, n), :] += term
 
-    def prepare(i, off, qq, lo, hi):
+    def bridge(c, w, hi):
+        first, last = srel[R - 1 : R, :], erel[R - 1 : R, :]
+        packed = []
+        for m, raw in enumerate(halves(dot_nt(q1[sl(0, hi), :], k1[sl(c, w), :]), w)):
+            allowed = (lanes(hi, (c + m) * CH - R) >= first) & (sublanes(hi, R) <= last)
+            packed.append(parts(raw, allowed)[0].astype(BF16))
+        term = dot_nn(joined(packed), v1[sl(c, w), :])
+        if hi == NC:
+            far[...] = term
+        else:
+            far[sl(0, hi), :] += term
+        for i in reversed(range(c, hi)):
+            o_out[sl(i), :] = far[sl(i), :].astype(BF16)
+            o_copies[i].start()
+
+    def far_slopes(c, w, hi):
+        for m, raw in enumerate(halves(dot_nt(qb[sl(0, hi), :], k2[sl(c, w), :]), w)):
+            allowed = lanes(hi, (c + m) * CH - 2 * R) >= srel[sl(0, hi), :]
+            fq[2, c + m, sl(0, hi), :] = parts(raw, allowed)[1]
+
+    def prepare(i, w, off, qq, lo, hi):
         n = hi - lo
-        raw = dot_nt(kb[sl(lo, n), :], qq[sl(i), :])
-        at = lanes(n, i * CH + off * R)
-        allowed = at <= erel[sl(lo, n), :]
-        if off == 0:
-            allowed = allowed & (at >= sublanes(n, lo * CH))
-        weights, slope = parts(raw)
-        ft[off, i, sl(lo, n), :] = jnp.where(allowed, slope, 0.0)
-        pt[off, i, sl(lo, n), :] = jnp.where(allowed, weights, 0.0).astype(BF16)
+        for m, raw in enumerate(halves(dot_nt(kb[sl(lo, n), :], qq[sl(i, w), :]), w)):
+            at = lanes(n, (i + m) * CH + off * R)
+            allowed = at <= erel[sl(lo, n), :]
+            if off == 0:
+                allowed = allowed & (at >= sublanes(n, lo * CH))
+            weights, slope = parts(raw, allowed)
+            ft[off, i + m, sl(lo, n), :] = slope
+            pt[off, i + m, sl(lo, n), :] = weights.astype(BF16)
 
     def stats_copies(c):
         return [
@@ -200,43 +229,40 @@
         def _():
             delta_copies[i][0].start()
 
-        @pl.when(has_left2)
-        def _():
-            delta_copies[i][1].start()
-
     def query_grad(c, off, kk, vv, lo, hi, fresh=False):
         n = hi - lo
-        pulled = dot_nt(d0[sl(lo, n), :], vv[sl(c), :])
-        grad = (pulled * fq[off, c, sl(lo, n), :]).astype(BF16)
-        term = dot_nn(grad, kk[sl(c), :])
+        pulled = dot_nt(d0[sl(lo, n), :], vv[sl(c, 2), :])
+        slope = joined([fq[off, c + m, sl(lo, n), :] for m in range(2)])
+        term = dot_nn((pulled * slope).astype(BF16), kk[sl(c, 2), :])
         if fresh:
             att[sl(lo, n), :] = term
         else:
             att[sl(lo, n), :] += term
 
-    def query_grads(lo, hi):
-        for c in range(hi):
-            query_grad(c, 0, kb, vb, max(lo, c), hi, fresh=c == 0)
+    def query_grads():
+        query_grad(0, 0, kb, vb, 0, NC, fresh=True)
+        query_grad(2, 0, kb, vb, 2, NC)
 
         @pl.when(has_left)
         def _():
-            for c in range(NC):
-                query_grad(c, 1, k1, v1, lo, hi)
+            query_grad(0, 1, k1, v1, 0, NC)
+            query_grad(2, 1, k1, v1, 0, NC)
 
         @pl.when(has_left2)
         def _():
-            for c in range(lo, NC):
-                query_grad(c, 2, k2, v2, lo, min(hi, c + 1))
-
-        gq_o[sl(lo, hi - lo), :] = (att[sl(lo, hi - lo), :] * factor).astype(BF16)
+            query_grad(0, 2, k2, v2, 0, 2)
+            query_grad(2, 2, k2, v2, 0, NC)
+
+        gq_o[...] = (att[...] * factor).astype(BF16)
 
     def key_grad(i, off, qq, dd, lo, hi, fresh=False):
         n = hi - lo
-        delta = dd[sl(i), :]
+        delta = dd[sl(i, 2), :]
         pulled = dot_nt(vb[sl(lo, n), :], delta)
-        grad = (pulled * ft[off, i, sl(lo, n), :]).astype(BF16)
-        key_add = dot_nn(grad, qq[sl(i), :])
-        value_add = dot_nn(pt[off, i, sl(lo, n), :], delta)
+        slope = joined([ft[off, i + m, sl(lo, n), :] for m in range(2)])
+        key_add = dot_nn((pulled * slope).astype(BF16), qq[sl(i, 2), :])
+        weights = joined([pt[off, i + m, sl(lo, n), :] for m in range(2)])
+        value_add = dot_nn(weights, delta)
         if fresh:
             dk[sl(lo, n), :] = key_add
             dv[sl(lo, n), :] = value_add
@@ -244,65 +270,104 @@
             dk[sl(lo, n), :] += key_add
             dv[sl(lo, n), :] += value_add
 
-    def remote_grads(i):
+    def relay(i):
         @pl.when(has_right)
         def _():
             delta_copies[i][0].wait_recv()
+
+            @pl.when(has_left)
+            def _():
+                delta_copies[i][1].start()
+
+    def near_grad(i):
+        @pl.when(has_right)
+        def _():
             key_grad(i, 1, q1, d1, 0, NC)
 
+    def far_grad(i):
         @pl.when(has_right2)
         def _():
-            delta_copies[i][1].wait_recv()
+            for c in (i, i + 1):
+                delta_copies[c][1].wait_recv()
             key_grad(i, 2, q2, d2, i, NC)
 
-    for c in range(NC):
-        forward(c, 0, kb, vb, c, NC, fresh=c == 0)
-    for i in range(NC):
-        prepare(i, 0, qb, 0, i + 1)
-    for c in reversed(range(NC)):
+    def arrive(c):
+        @pl.when(has_left2)
+        def _():
+            o_copies[c].wait_recv()
+            att[sl(c), :] += o_in[sl(c), :].astype(F32)
+
+        stats_send(c)
+
+    def far_arrive():
+        @pl.when(has_left2)
+        def _():
+            for c in reversed(range(NC)):
+                for copy in kv2[c]:
+                    copy.wait_recv()
+            far_slopes(2, 2, NC)
+            far_slopes(0, 2, 2)
+
+    forward(0, 2, 0, kb, vb, 0, NC, fresh=True)
+    forward(2, 2, 0, kb, vb, 2, NC)
+    prepare(0, 2, 0, qb, 0, 2)
+    prepare(2, 2, 0, qb, 0, NC)
+
+    @pl.when(has_right)
+    def _():
+        q_copies[0].wait_recv()
+
         @pl.when(has_left)
         def _():
-            for copy in kv1[c]:
-                copy.wait_recv()
+            q_copies[1].start()
+
+    for c, w in ((2, 2), (1, 1), (0, 1)):
+        @pl.when(has_left)
+        def _():
+            for m in range(w):
+                for copy in kv1[c + m]:
+                    copy.wait_recv()
 
             @pl.when(has_right)
             def _():
-                for copy in kv2[c]:
-                    copy.start()
-
-            forward(c, 1, k1, v1, 0, NC)
+                bridge(c, w, c + w)
+
+            forward(c, w, 1, k1, v1, 0, NC)
+
+    @pl.when(has_left & has_right)
+    def _():
+        for c in reversed(range(NC)):
+            for copy in kv2[c]:
+                copy.start()
+
+    for c in reversed(range(NC)):
+        arrive(c)
 
     @pl.when(has_right)
     def _():
-        q_copies[0].wait_recv()
-        for i in range(NC):
-            prepare(i, 1, q1, 0, NC)
+        prepare(0, 2, 1, q1, 0, NC)
+        prepare(2, 2, 1, q1, 0, NC)
 
     @pl.when(has_right2)
     def _():
         q_copies[1].wait_recv()
-        for i in range(NC):
-            prepare(i, 2, q2, i, NC)
+        prepare(0, 2, 2, q2, 0, NC)
+        prepare(2, 2, 2, q2, 2, NC)
 
     for c in reversed(range(NC)):
-        @pl.when(has_left2)
-        def _():
-            for copy in kv2[c]:
-                copy.wait_recv()
-            forward(c, 2, k2, v2, 0, c + 1)
-
-        stats_send(c)
-        if c + 1 < NC:
-            stats_use(c + 1)
-            key_grad(c + 1, 0, qb, d0, 0, c + 2, fresh=c + 1 == NC - 1)
-    query_grads(NC // 2, NC)
-    for i in reversed(range(NC // 2, NC)):
-        remote_grads(i)
-    stats_use(0)
-    key_grad(0, 0, qb, d0, 0, 1)
-    query_grads(0, NC // 2)
-    for i in reversed(range(NC // 2)):
-        remote_grads(i)
+        stats_use(c)
+    relay(3)
+    key_grad(2, 0, qb, d0, 0, NC, fresh=True)
+    relay(2)
+    key_grad(0, 0, qb, d0, 0, 2)
+    relay(1)
+    near_grad(2)
+    relay(0)
+    near_grad(0)
+    far_arrive()
+    query_grads()
+    far_grad(2)
+    far_grad(0)
     gk_o[...] = (dk[...] * factor).astype(BF16)
     gv_o[...] = dv[...].astype(BF16)
 
@@ -315,15 +380,21 @@
     @pl.when(has_left & has_right)
     def _():
         for c in range(NC):
+            o_copies[c].wait_send()
             for copy in kv2[c]:
                 copy.wait_send()
 
-    for n, there in enumerate((has_left, has_left2)):
-        @pl.when(there)
-        def _():
-            q_copies[n].wait_send()
-            for c in range(NC):
-                delta_copies[c][n].wait_send()
+    @pl.when(has_left)
+    def _():
+        q_copies[0].wait_send()
+        for c in range(NC):
+            delta_copies[c][0].wait_send()
+
+    @pl.when(has_left & has_right)
+    def _():
+        q_copies[1].wait_send()
+        for c in range(NC):
+            delta_copies[c][1].wait_send()
 
     for c in range(NC):
         for copy in stats_copies(c):
@@ -359,11 +430,12 @@
             pltpu.VMEM((2, R), jnp.int32),
             *[bf(*block)] * 5,
             *[bf(*block)] * 9,
+            fl(*block), bf(*block), bf(*block),
             pltpu.VMEM((R, CH), jnp.int32), pltpu.VMEM((R, CH), jnp.int32),
             fl(3, NC, R, CH), fl(3, NC, R, CH), bf(3, NC, R, CH),
             fl(*block), fl(*block), fl(*block),
             fl(NC, 8, CH), fl(heads_n, NC, 8, CH),
-            dma(6), dma(2, NC), dma(2, NC), dma(2, NC), dma(2, NC),
+            dma(6), dma(2, NC), dma(2, NC), dma(2, NC), dma(2, NC), dma(NC), dma(NC),
             dma(2), dma(2), dma(2, NC), dma(2, NC),
             dma(heads_n - 1, NC), dma(heads_n, NC),
         ],

time: 38.6 us -> 35.3 us (0.915)
  Pallas kernels: 37.8 us -> 34.5 us
    pallas_call x1, Pallas kernels: 37 us -> 33.7 us  [local(): pl.pallas_call(functools.partial(kernel, rows_n, heads_n, DH ** (-0.5)),...]
where the time goes in v3:
time: 35.3 us; the launch traced here: 35.2 us
  Pallas kernels  34.5 us (98%)
  between operations  0.64 us (2%)
    pallas_call x1, Pallas kernels, local(): pl.pallas_call(functools.partial(kernel, rows_n, heads_n, DH ** (-0.5)),...  33.7 us
    pallas_call x1, Pallas kernels, local(): pl.pallas_call(store_kernel, out_shape=(out,) * 5, in_specs=[pl.BlockSpec...  0.87 us

profile of v3, /device:TPU:1, one launch (start us, length us, event | category | flops | bytes accessed | tf_op | source)
XLA Modules:
  0.0 35.2 jit_solution(1153251787810892325)
XLA Ops:
  0.6 33.7 %jagged_attention.1 = (bf16[512,128]{1,0:T(8,128)(2,1)S(1)}, bf16[512,128]{1,0:T(8,128)(2,1)S(1)}, bf16[512,128]{1,0:T(8,128)(2,1)S(1)}, bf16[512,128]{1,0:T(8,128)(2,1)S(1)}, bf16[512,128]{1,0:T(8,128)(2,1)S(1)}) custom-call(s32[2,512]{1,0:T(2,128)} %bounds_h.1, bf16[512,128]{1,0:T(8,128)(2,1)} %q_h.1, bf16[512,128]{1,0:T(8,128)(2,1)} %k_h.1, ...), custom_call_target="tpu_custom_call" | custom-call | tf_op jit(solution)/shard_map/jagged_attention/pallas_call | solution.py:424
  34.3 0.9 %store_outputs.1 = (bf16[512,128]{1,0:T(8,128)(2,1)}, bf16[512,128]{1,0:T(8,128)(2,1)}, bf16[512,128]{1,0:T(8,128)(2,1)}, bf16[512,128]{1,0:T(8,128)(2,1)}, bf16[512,128]{1,0:T(8,128)(2,1)}) custom-call(bf16[512,128]{1,0:T(8,128)(2,1)S(1)} %get-tuple-element.10.refs_0_, bf16[512,128]{1,0:T(8,128)(2,1)S(1)} %get-tuple-element.11.refs_1_, ...), custom_call_target="tpu_custom_call" | custom-call | tf_op jit(solution)/shard_map/store_outputs/pallas_call | solution.py:445

commit v4 on v3

--- a/solution.py
+++ b/solution.py
@@ -9,6 +9,8 @@
 
 DH = 128
 CH = 128
+USHER = 2
+LAZY = (1,)
 LOG2E = 1.4426950408889634
 MASKED = -1e30
 EPSILON = 1e-05
@@ -32,7 +34,7 @@
     bnd, qb, kb, vb, gb, cb,
     k1, v1, k2, v2, q1, q2, d0, d1, d2, far, o_out, o_in,
     srel, erel, fq, ft, pt, att, dk, dv, st_out, st_in,
-    lsem, s1, r1, s2, r2, so, ro, sq, rq, sd, rd, ss, rs,
+    lsem, s1, r1, s2, r2, so, ro, sq, rq, sd, rd, ss, rs, usher_sem, left_sem,
 ):
     R = q_h.shape[0]
     NC = R // CH
@@ -48,13 +50,18 @@
     def sl(c, n=1):
         return pl.ds(c * CH, n * CH)
 
+    lazy_left = functools.reduce(jnp.logical_or, [pos == row for row in LAZY])
+    lazy_right = functools.reduce(jnp.logical_or, [pos == row - 1 for row in LAZY])
     barrier = pltpu.get_barrier_semaphore()
-    for there, who in ((has_left, left), (has_right, right)):
+    for there, who in ((has_left, left), (has_right & ~lazy_right, right)):
         @pl.when(there)
         def _():
             pl.semaphore_signal(barrier, inc=1, device_id={"rows": who}, device_id_type=MESH)
+
     for who in peers:
-        pl.semaphore_signal(barrier, inc=1, device_id={"heads": who}, device_id_type=MESH)
+        @pl.when((head != 0) | (who == USHER))
+        def _():
+            pl.semaphore_signal(barrier, inc=1, device_id={"heads": who}, device_id_type=MESH)
     loads = [
         pltpu.make_async_copy(src, dst, lsem.at[n])
         for n, (src, dst) in enumerate(
@@ -63,8 +70,9 @@
     ]
     for copy in loads:
         copy.start()
-    greeters = has_left.astype(jnp.int32) + has_right.astype(jnp.int32)
-    pl.semaphore_wait(barrier, greeters + len(peers))
+    greeters = has_right.astype(jnp.int32) + (has_left & ~lazy_left).astype(jnp.int32)
+    ushered = (head != 0) & (head != USHER)
+    pl.semaphore_wait(barrier, greeters + len(peers) - ushered.astype(jnp.int32))
 
     def remote(src, dst, send, recv, **who):
         return pltpu.make_async_remote_copy(
@@ -100,6 +108,21 @@
         for c in reversed(range(NC)):
             for copy in kv1[c]:
                 copy.start()
+
+    @pl.when(lazy_right)
+    def _():
+        pl.semaphore_signal(left_sem, inc=1, device_id={"rows": right}, device_id_type=MESH)
+
+    @pl.when(head == USHER)
+    def _():
+        for who in peers:
+            @pl.when(who != 0)
+            def _():
+                pl.semaphore_signal(usher_sem, inc=1, device_id={"heads": who}, device_id_type=MESH)
+
+    @pl.when(lazy_left)
+    def _():
+        pl.semaphore_wait(left_sem, 1)
 
     @pl.when(has_left)
     def _():
@@ -239,10 +262,11 @@
         else:
             att[sl(lo, n), :] += term
 
-    def query_grads():
+    def query_own():
         query_grad(0, 0, kb, vb, 0, NC, fresh=True)
         query_grad(2, 0, kb, vb, 2, NC)
 
+    def query_far():
         @pl.when(has_left)
         def _():
             query_grad(0, 1, k1, v1, 0, NC)
@@ -340,6 +364,10 @@
             for copy in kv2[c]:
                 copy.start()
 
+    @pl.when(ushered)
+    def _():
+        pl.semaphore_wait(usher_sem, 1)
+
     for c in reversed(range(NC)):
         arrive(c)
 
@@ -356,8 +384,9 @@
 
     for c in reversed(range(NC)):
         stats_use(c)
+    key_grad(2, 0, qb, d0, 0, NC, fresh=True)
     relay(3)
-    key_grad(2, 0, qb, d0, 0, NC, fresh=True)
+    query_own()
     relay(2)
     key_grad(0, 0, qb, d0, 0, 2)
     relay(1)
@@ -365,7 +394,7 @@
     relay(0)
     near_grad(0)
     far_arrive()
-    query_grads()
+    query_far()
     far_grad(2)
     far_grad(0)
     gk_o[...] = (dk[...] * factor).astype(BF16)
@@ -437,7 +466,7 @@
             fl(NC, 8, CH), fl(heads_n, NC, 8, CH),
             dma(6), dma(2, NC), dma(2, NC), dma(2, NC), dma(2, NC), dma(NC), dma(NC),
             dma(2), dma(2), dma(2, NC), dma(2, NC),
-            dma(heads_n - 1, NC), dma(heads_n, NC),
+            dma(heads_n - 1, NC), dma(heads_n, NC), pltpu.SemaphoreType.REGULAR, pltpu.SemaphoreType.REGULAR,
         ],
         compiler_params=pltpu.CompilerParams(collective_id=0, has_side_effects=True),
         name="jagged_attention",

time: 35.3 us -> 33.9 us (0.960)
  the two profiles are of different devices: /device:TPU:1 before, /device:TPU:496 now
where the time goes in v4:
time: 33.9 us; the launch traced here: 33.8 us
  Pallas kernels  33.1 us (98%)
  between operations  0.64 us (2%)
    pallas_call x1, Pallas kernels, local(): pl.pallas_call(functools.partial(kernel, rows_n, heads_n, DH ** (-0.5)),...  32.3 us
    pallas_call x1, Pallas kernels, local(): pl.pallas_call(store_kernel, out_shape=(out,) * 5, in_specs=[pl.BlockSpec...  0.87 us

profile of v4, /device:TPU:496, one launch (start us, length us, event | category | flops | bytes accessed | tf_op | source)
XLA Modules:
  0.0 33.8 jit_solution(8880954366550558908)
XLA Ops:
  0.6 32.3 %jagged_attention.1 = (bf16[512,128]{1,0:T(8,128)(2,1)S(1)}, bf16[512,128]{1,0:T(8,128)(2,1)S(1)}, bf16[512,128]{1,0:T(8,128)(2,1)S(1)}, bf16[512,128]{1,0:T(8,128)(2,1)S(1)}, bf16[512,128]{1,0:T(8,128)(2,1)S(1)}) custom-call(s32[2,512]{1,0:T(2,128)} %bounds_h.1, bf16[512,128]{1,0:T(8,128)(2,1)} %q_h.1, bf16[512,128]{1,0:T(8,128)(2,1)} %k_h.1, ...), custom_call_target="tpu_custom_call" | custom-call | tf_op jit(solution)/shard_map/jagged_attention/pallas_call | solution.py:453
  32.9 0.9 %store_outputs.1 = (bf16[512,128]{1,0:T(8,128)(2,1)}, bf16[512,128]{1,0:T(8,128)(2,1)}, bf16[512,128]{1,0:T(8,128)(2,1)}, bf16[512,128]{1,0:T(8,128)(2,1)}, bf16[512,128]{1,0:T(8,128)(2,1)}) custom-call(bf16[512,128]{1,0:T(8,128)(2,1)S(1)} %get-tuple-element.10.refs_0_, bf16[512,128]{1,0:T(8,128)(2,1)S(1)} %get-tuple-element.11.refs_1_, ...), custom_call_target="tpu_custom_call" | custom-call | tf_op jit(solution)/shard_map/store_outputs/pallas_call | solution.py:474

commit v5 on v4

--- a/solution.py
+++ b/solution.py
@@ -337,6 +337,13 @@
     prepare(0, 2, 0, qb, 0, 2)
     prepare(2, 2, 0, qb, 0, NC)
 
+    @pl.when(has_left)
+    def _():
+        for m in (3, 2):
+            for copy in kv1[m]:
+                copy.wait_recv()
+        forward(2, 2, 1, k1, v1, 0, NC)
+
     @pl.when(has_right)
     def _():
         q_copies[0].wait_recv()
@@ -344,19 +351,19 @@
         @pl.when(has_left)
         def _():
             q_copies[1].start()
-
-    for c, w in ((2, 2), (1, 1), (0, 1)):
+            bridge(2, 2, NC)
+
+    for c in (1, 0):
         @pl.when(has_left)
         def _():
-            for m in range(w):
-                for copy in kv1[c + m]:
-                    copy.wait_recv()
+            for copy in kv1[c]:
+                copy.wait_recv()
 
             @pl.when(has_right)
             def _():
-                bridge(c, w, c + w)
-
-            forward(c, w, 1, k1, v1, 0, NC)
+                bridge(c, 1, c + 1)
+
+            forward(c, 1, 1, k1, v1, 0, NC)
 
     @pl.when(has_left & has_right)
     def _():
@@ -376,15 +383,16 @@
         prepare(0, 2, 1, q1, 0, NC)
         prepare(2, 2, 1, q1, 0, NC)
 
+    for c in reversed(range(NC)):
+        stats_use(c)
+    key_grad(2, 0, qb, d0, 0, NC, fresh=True)
+
     @pl.when(has_right2)
     def _():
         q_copies[1].wait_recv()
         prepare(0, 2, 2, q2, 0, NC)
         prepare(2, 2, 2, q2, 2, NC)
 
-    for c in reversed(range(NC)):
-        stats_use(c)
-    key_grad(2, 0, qb, d0, 0, NC, fresh=True)
     relay(3)
     query_own()
     relay(2)

time: 33.9 us -> 33.1 us (0.976)
  the two profiles are of different devices: /device:TPU:496 before, /device:TPU:1 now
where the time goes in v5:
time: 33.1 us; the launch traced here: 32.8 us
  Pallas kernels  32.1 us (97%)
  between operations  0.64 us (2%)
    pallas_call x1, Pallas kernels, local(): pl.pallas_call(functools.partial(kernel, rows_n, heads_n, DH ** (-0.5)),...  31.2 us
    pallas_call x1, Pallas kernels, local(): pl.pallas_call(store_kernel, out_shape=(out,) * 5, in_specs=[pl.BlockSpec...  0.87 us

profile of v5, /device:TPU:1, one launch (start us, length us, event | category | flops | bytes accessed | tf_op | source)
XLA Modules:
  0.0 32.8 jit_solution(1600643444727385388)
XLA Ops:
  0.6 31.2 %jagged_attention.1 = (bf16[512,128]{1,0:T(8,128)(2,1)S(1)}, bf16[512,128]{1,0:T(8,128)(2,1)S(1)}, bf16[512,128]{1,0:T(8,128)(2,1)S(1)}, bf16[512,128]{1,0:T(8,128)(2,1)S(1)}, bf16[512,128]{1,0:T(8,128)(2,1)S(1)}) custom-call(s32[2,512]{1,0:T(2,128)} %bounds_h.1, bf16[512,128]{1,0:T(8,128)(2,1)} %q_h.1, bf16[512,128]{1,0:T(8,128)(2,1)} %k_h.1, ...), custom_call_target="tpu_custom_call" | custom-call | tf_op jit(solution)/shard_map/jagged_attention/pallas_call | solution.py:461
  31.9 0.9 %store_outputs.1 = (bf16[512,128]{1,0:T(8,128)(2,1)}, bf16[512,128]{1,0:T(8,128)(2,1)}, bf16[512,128]{1,0:T(8,128)(2,1)}, bf16[512,128]{1,0:T(8,128)(2,1)}, bf16[512,128]{1,0:T(8,128)(2,1)}) custom-call(bf16[512,128]{1,0:T(8,128)(2,1)S(1)} %get-tuple-element.10.refs_0_, bf16[512,128]{1,0:T(8,128)(2,1)S(1)} %get-tuple-element.11.refs_1_, ...), custom_call_target="tpu_custom_call" | custom-call | tf_op jit(solution)/shard_map/store_outputs/pallas_call | solution.py:482
